TPU v7x, 256 devices: a whole 4x4x8 slice. The times are simulated.
256 devices in a mesh: row: 32 (over z_hi, y, core), col: 8 (over z_lo, x).
Axes of the slice: x: 4, y: 4, z: 8 (z_hi: 4, z_lo: 2; z = z_hi * 2 + z_lo), core: 2. Of those that a mesh axis runs over, the one named last changes fastest.
Arguments:
- left: float32 [128, 16384], P('col', 'row'), may hold values from -12 to 12
- right: float32 [128, 16384], P('row', 'col'), may hold values from -12 to 12
- w_out: float32 [1024, 128], replicated, may hold values from -0.1875 to 0.1875
- b_out: float32 [128], replicated, may hold values from -3 to 3
- pair_grad: float32 [512, 512, 128], P('row', 'col'), may hold values from -6 to 6
Outputs:
- pair_out: float32 [512, 512, 128], P('row', 'col')
- grad_left: float32 [128, 16384], P('col', 'row')
- grad_right: float32 [128, 16384], P('row', 'col')
- grad_weight: float32 [1024, 128], replicated
- grad_bias: float32 [128], replicated
All inputs are finite; a program needn't handle non-finite values.
Results may differ from a plain program's by a relative error of at most 0.0001.
Values sent between devices are 32-bit elements; how exact they have to be, the bound alone decides.
No kernel may reach another device: no remote copies, remote signals or barrier semaphores. Data moves between devices by JAX's collectives and lax.ppermute only.
A program may use at most 128 MiB of HBM per device.

v0:
```python
import jax
import jax.numpy as jnp
from jax import lax
from jax.sharding import PartitionSpec as P

C = 32
Z = 128
S = 128


def body(left, right, w_out, b_out, pair_grad):
    highest = lax.Precision.HIGHEST
    tile_rows = left.shape[1] // C
    tile_cols = right.shape[1] // C
    residues = tile_rows * lax.axis_size("row")
    weight_cube = w_out.reshape(C, C, Z)
    contract_rows = (((0,), (0,)), ((), ()))
    contract_cols = (((1,), (1,)), ((), ()))
    left_all = lax.all_gather(left, "col", axis=0, tiled=True)
    right_all = lax.all_gather(right, "row", axis=0, tiled=True)
    outer = (
        lax.dot_general(
            left_all,
            right_all,
            contract_rows,
            precision=highest,
            preferred_element_type=jnp.float32,
        )
        / S
    )
    outer_split = outer.reshape(tile_rows, C, tile_cols, C)
    pair_out = jnp.einsum("icje,cez->ijz", outer_split, weight_cube, precision=highest) + b_out
    grad_outer = jnp.einsum("ijz,cez->icje", pair_grad, weight_cube, precision=highest)
    grad_outer = grad_outer.reshape(tile_rows * C, tile_cols * C)
    grad_left = lax.psum_scatter(
        lax.dot_general(
            right_all,
            grad_outer,
            contract_cols,
            precision=highest,
            preferred_element_type=jnp.float32,
        )
        / S,
        "col",
        scatter_dimension=0,
        tiled=True,
    )
    grad_right = lax.psum_scatter(
        jnp.dot(left_all, grad_outer, precision=highest) / S, "row", scatter_dimension=0, tiled=True
    )
    weight_term = jnp.einsum("icje,ijz->cez", outer_split, pair_grad, precision=highest).reshape(
        C * C, Z
    )
    bias_term = jnp.sum(pair_grad, axis=(0, 1))
    grad_weight, grad_bias = lax.psum((weight_term, bias_term), ("row", "col"))
    return (pair_out, grad_left, grad_right, grad_weight / residues, grad_bias / residues)


def solution(mesh):
    placed = (P("col", "row"), P("row", "col"), P(), P(), P("row", "col", None))
    return jax.shard_map(
        body,
        mesh=mesh,
        in_specs=placed,
        out_specs=(P("row", "col", None), P("col", "row"), P("row", "col"), P(), P()),
        check_vma=False,
    )
```

profile of v0, /device:TPU:8, one launch (start us, length us, event | category | flops | bytes accessed | tf_op | source)
XLA Modules:
  0.0 770.1 jit_solution(7213743941106208333)
XLA Ops:
  7.2 29.5 %all_gather.6 = f32[128,512]{1,0:T(8,128)S(1)} all-gather(f32[16,512]{1,0:T(8,128)} %param.5), channel_id=1, replica_groups=mesh['row'=32,'col'=8] {'col'}, dimensions={0}, use_global_device_ids=true | all-gather | bytes 294912 | tf_op jit(solution)/shard_map/all_gather | solution.py:19
  36.8 9.8 %convolution_bitcast_fusion = f32[16,32,64,32]{2,3,0,1:T(8,128)} fusion(f32[32,32,128,1]{2,1,3,0:T(8,128)S(1)} %bitcast.42, f32[16,64,128]{2,1,0:T(8,128)} %param.9), kind=kOutput, calls=%fused_computation.1 | convolution fusion | flops 1610612736 | bytes 5242880 | tf_op jit(solution)/shard_map/ijz,cez->icje/dot_general | solution.py:33
  46.6 12.3 %copy.21 = f32[16,32,64,32]{3,2,1,0:T(8,128)} copy(f32[16,32,64,32]{2,3,0,1:T(8,128)} %convolution_bitcast_fusion) | data formatting | bytes 8388608 | tf_op jit(solution)/shard_map/ijz,cez->icje/transpose | solution.py:33
  58.9 13.5 %reshape.24 = f32[512,2048]{1,0:T(8,128)} reshape(f32[16,32,64,32]{3,2,1,0:T(8,128)} %copy.21) | data formatting | bytes 8388608 | tf_op jit(solution)/shard_map/reshape | solution.py:34
  72.4 9.9 %fusion = f32[128,2048]{0,1:T(8,128)} fusion(f32[512,2048]{1,0:T(8,128)} %reshape.24, f32[128,512]{1,0:T(8,128)S(1)} %all_gather.6), kind=kOutput, calls=%fused_computation.3 | convolution fusion | flops 1610874880 | bytes 5505024 | tf_op jit(solution)/shard_map/dot_general | solution.py:49
  82.3 0.7 all-gather.3.cloned.1.call-update
  83.4 0.6 dynamic-slice
  84.7 77.5 %psum.15 = f32[128]{0:T(128)S(1)} all-reduce(f32[128]{0:T(128)S(1)} %reduce_sum.9), channel_id=1, replica_groups=mesh['row'=32,'col'=8] {'row','col'}, use_global_device_ids=true, to_apply=%region_4.0 | all-reduce | flops 128 | bytes 1024 | tf_op jit(solution)/shard_map/psum | solution.py:55
  162.1 0.5 broadcast_multiply_fusion.1
  162.6 205.9 %all-reduce.6.cloned.1.call-done = f32[128,2048]{0,1:T(8,128)} async-done(((f32[128,2048]{0,1:T(8,128)}), f32[128,2048]{0,1:T(8,128)}) %all-reduce.6.cloned.1.call-update) | async-done | bytes 1048592
  368.6 1.6 constant_dynamic-slice_fusion
  370.1 0.9 copy.25
  371.1 55.6 %all-gather.3.cloned.1.call-done = f32[32,4,2048]{2,1,0:T(4,128)} async-done(((f32[1,4,2048]{2,1,0:T(4,128)}), f32[32,4,2048]{2,1,0:T(4,128)}) %all-gather.3.cloned.1.call-update) | async-done | bytes 1048592 | tf_op jit(solution)/shard_map/all_gather | solution.py:20
  426.7 1.6 reshape.26
  428.3 5.0 convolution_multiply_fusion
  433.3 11.4 %reshape.22 = f32[16,32,64,32]{3,2,1,0:T(8,128)} reshape(f32[512,2048]{1,0:T(8,128)} %convolution_multiply_fusion) | data formatting | bytes 8388608 | tf_op jit(solution)/shard_map/reshape | solution.py:31
  444.7 12.7 %copy.33 = f32[32,32,16,64]{3,1,0,2:T(8,128)} copy(f32[32,32,16,64]{1,3,0,2:T(8,128)} %bitcast.44) | data formatting | bytes 8388608 | tf_op jit(solution)/shard_map/icje,ijz->cez/dot_general | solution.py:51
  457.4 9.9 %convolution_bitcast_fusion.2 = f32[1024,128]{1,0:T(8,128)} fusion(f32[1024,16,64]{2,0,1:T(8,128)} %bitcast.45, f32[16,64,128]{2,1,0:T(8,128)S(1)} %copy-done.1), kind=kOutput, calls=%fused_computation.5 | convolution fusion | flops 1610612736 | bytes 5242880 | tf_op jit(solution)/shard_map/icje,ijz->cez/dot_general | solution.py:51
  467.6 5.2 fusion.2
  472.8 0.8 copy.29
  473.7 17.6 %fusion.1 = f32[16,64,128]{2,1,0:T(8,128)} fusion(f32[16,32,64,32]{3,2,1,0:T(8,128)} %reshape.22, f32[32,32,128,1]{2,1,0,3:T(8,128)S(1)} %bitcast.43, f32[128]{0:T(128)S(1)} %copy-done.2), kind=kOutput, calls=%fused_computation.6 | convolution fusion | flops 1610743808 | bytes 5243392 | tf_op jit(solution)/shard_map/icje,cez->ijz/dot_general | solution.py:32
  491.3 230.2 %all-reduce.4.cloned.1.call-done = f32[1024,128]{1,0:T(8,128)} async-done(((f32[1024,128]{1,0:T(8,128)}), f32[1024,128]{1,0:T(8,128)}) %all-reduce.4.cloned.1.call-update) | async-done | bytes 524304 | tf_op jit(solution)/shard_map/psum | solution.py:55
  721.5 1.9 broadcast_multiply_fusion
  723.4 40.2 %reduce-scatter.5.cloned.1.call-done = f32[16,512]{1,0:T(8,128)} async-done(((f32[128,512]{1,0:T(8,128)}), f32[16,512]{1,0:T(8,128)}) %reduce-scatter.5.cloned.1.call-update) | async-done | bytes 32784
  (16 shorter events, 0.8 us)
Async XLA Ops:
  7.2 29.6 %copy-start = (f32[1024,128]{1,0:T(8,128)S(1)}, f32[1024,128]{1,0:T(8,128)}, u32[]{:S(2)}) copy-start(f32[1024,128]{1,0:T(8,128)} %param.7) | copy-start | bytes 1572868
  7.2 361.4 %all-reduce.6.cloned.1.call-start = ((), (), s32[]{:S(2)}) async-start(), calls=%async_computation.4 | async-start | bytes 2097152
  58.9 24.3 %copy-start.1 = (f32[16,64,128]{2,1,0:T(8,128)S(1)}, f32[16,64,128]{2,1,0:T(8,128)}, u32[]{:S(2)}) copy-start(f32[16,64,128]{2,1,0:T(8,128)} %param.9) | copy-start | bytes 1572868
  58.9 24.5 %copy-start.3 = (u32[256]{0:T(256)S(1)}, u32[256]{0:T(256)}, u32[]{:S(2)}) copy-start(u32[256]{0:T(256)} %constant.18) | copy-start | bytes 3076
  82.3 344.4 %all-gather.3.cloned.1.call-start = ((), (), s32[]{:S(2)}) async-start(), calls=%async_computation.2 | async-start | bytes 1081344 | tf_op jit(solution)/shard_map/all_gather | solution.py:20
  83.0 638.5 %all-reduce.4.cloned.1.call-start = ((), (), s32[]{:S(2)}) async-start(), calls=%async_computation.1 | async-start | bytes 1048576 | tf_op jit(solution)/shard_map/psum | solution.py:55
  457.4 16.3 %copy-start.2 = (f32[128]{0:T(128)S(1)}, f32[128]{0:T(128)}, u32[]{:S(2)}) copy-start(f32[128]{0:T(128)} %param.8) | copy-start | bytes 1540
  467.3 296.3 %reduce-scatter.5.cloned.1.call-start = ((), (), s32[]{:S(2)}) async-start(), calls=%async_computation.3 | async-start | bytes 294912
Sparse Core Ops, SparseCore 0:
  82.4 286.1 all-reduce.5
  371.1 55.5 all-gather.2
  467.4 254.0 all-reduce.3
  724.4 39.1 reduce-scatter.4
where the time goes:
time: 771 us; the launch traced here: 770 us
  waiting for transfers between devices  533 us (69%)
  blocking collectives  107 us (14%)
  matrix products  57.4 us (7%)
  local copies, waits for them, and re-layouts  55.4 us (7%)
  between operations  14.5 us (2%)
    unnamed x6, waiting for transfers between devices  247 us
    psum x1, waiting for transfers between devices, body(): grad_weight, grad_bias = lax.psum((weight_term, bias_term), ('row', 'col'))  230 us
    psum x1, blocking collectives, body(): grad_weight, grad_bias = lax.psum((weight_term, bias_term), ('row', 'col'))  77.5 us
    all_gather x1, waiting for transfers between devices, body(): right_all = lax.all_gather(right, 'row', axis=0, tiled=True)  55.6 us
    all_gather x1, blocking collectives, body(): left_all = lax.all_gather(left, 'col', axis=0, tiled=True)  29.5 us
    dot_general x1, matrix products, body(): jnp.einsum('icje,cez->ijz', outer_split, weight_cube, precision=highest)  17.6 us
  transfers between devices with their start and end apart: 4, of which 4 were waited for; matrix products, arithmetic and copies ran while one was open for 4% of the time, Pallas kernels for 0%

commit v1 on v0

--- a/solution.py
+++ b/solution.py
@@ -17,7 +17,9 @@
     contract_rows = (((0,), (0,)), ((), ()))
     contract_cols = (((1,), (1,)), ((), ()))
     left_all = lax.all_gather(left, "col", axis=0, tiled=True)
-    right_all = lax.all_gather(right, "row", axis=0, tiled=True)
+    right_all = jnp.concatenate(
+        lax.all_to_all(jnp.stack([right] * lax.axis_size("row")), "row", 0, 0), axis=0
+    )
     outer = (
         lax.dot_general(
             left_all,

time: 771 us -> 734 us (0.952)
  waiting for transfers between devices: 533 us -> 484 us
  starting transfers between devices: 0.56 us -> 12.1 us
    all_gather x1 -> x0, waiting for transfers between devices: 55.6 us -> none  [body(): right_all = lax.all_gather(right, 'row', axis=0, tiled=True)]
    all_to_all x0 -> x1, starting transfers between devices: none -> 11.7 us  [body(): lax.all_to_all(jnp.stack([right] * lax.axis_size('row')), 'row', 0, 0)]
    unnamed x6 -> x5, waiting for transfers between devices: 247 us -> 248 us
  transfers between devices with their start and end apart: 4 -> 4, of which waited for: 4 -> 3; matrix products, arithmetic and copies ran while one was open for 4% -> 10% of each run, Pallas kernels for 0% -> 0%
where the time goes in v1:
time: 734 us; the launch traced here: 732 us
  waiting for transfers between devices  484 us (66%)
  blocking collectives  104 us (14%)
  matrix products  57.4 us (8%)
  local copies, waits for them, and re-layouts  56.3 us (8%)
  between operations  16.2 us (2%)
  starting transfers between devices  12.1 us (2%)
    unnamed x5, waiting for transfers between devices  248 us
    psum x1, waiting for transfers between devices, body(): grad_weight, grad_bias = lax.psum((weight_term, bias_term), ('row', 'col'))  236 us
    psum x1, blocking collectives, body(): grad_weight, grad_bias = lax.psum((weight_term, bias_term), ('row', 'col'))  75.8 us
    all_gather x1, blocking collectives, body(): left_all = lax.all_gather(left, 'col', axis=0, tiled=True)  28.6 us
    dot_general x1, matrix products, body(): jnp.einsum('icje,cez->ijz', outer_split, weight_cube, precision=highest)  17.6 us
  transfers between devices with their start and end apart: 4, of which 3 were waited for; matrix products, arithmetic and copies ran while one was open for 10% of the time, Pallas kernels for 0%

profile of v1, /device:TPU:8, one launch (start us, length us, event | category | flops | bytes accessed | tf_op | source)
XLA Modules:
  0.0 732.5 jit_solution(11603031145558736444)
XLA Ops:
  8.0 2.1 stack.2
  10.1 11.7 %all-to-all-start = ((f32[32,4,2048]{2,1,0:T(4,128)}), f32[32,4,2048]{2,1,0:T(4,128)S(1)}, u32[]{:S(2)}, u32[]{:S(2)}) async-start(f32[32,4,2048]{2,1,0:T(4,128)} %stack.2), calls=%async_computation | async-start | bytes 2097152 | tf_op jit(solution)/shard_map/all_to_all | solution.py:21
  21.9 9.8 %convolution_bitcast_fusion = f32[16,32,64,32]{2,3,0,1:T(8,128)} fusion(f32[32,32,128,1]{2,1,3,0:T(8,128)S(1)} %bitcast.42, f32[16,64,128]{2,1,0:T(8,128)} %param.9), kind=kOutput, calls=%fused_computation.1 | convolution fusion | flops 1610612736 | bytes 5242880 | tf_op jit(solution)/shard_map/ijz,cez->icje/dot_general | solution.py:35
  31.7 12.3 %copy.21 = f32[16,32,64,32]{3,2,1,0:T(8,128)} copy(f32[16,32,64,32]{2,3,0,1:T(8,128)} %convolution_bitcast_fusion) | data formatting | bytes 8388608 | tf_op jit(solution)/shard_map/ijz,cez->icje/transpose | solution.py:35
  44.0 13.5 %reshape.30 = f32[512,2048]{1,0:T(8,128)} reshape(f32[16,32,64,32]{3,2,1,0:T(8,128)} %copy.21) | data formatting | bytes 8388608 | tf_op jit(solution)/shard_map/reshape | solution.py:36
  57.5 28.6 %all_gather.3 = f32[128,512]{1,0:T(8,128)S(1)} all-gather(f32[16,512]{1,0:T(8,128)S(1)} %copy-done.2), channel_id=1, replica_groups=mesh['row'=32,'col'=8] {'col'}, dimensions={0}, use_global_device_ids=true | all-gather | bytes 294912 | tf_op jit(solution)/shard_map/all_gather | solution.py:19
  86.1 9.9 %fusion = f32[128,2048]{0,1:T(8,128)} fusion(f32[512,2048]{1,0:T(8,128)} %reshape.30, f32[128,512]{1,0:T(8,128)S(1)} %all_gather.3), kind=kOutput, calls=%fused_computation.3 | convolution fusion | flops 1610874880 | bytes 5505024 | tf_op jit(solution)/shard_map/dot_general | solution.py:51
  96.2 0.6 dynamic-slice
  97.4 75.8 %psum.15 = f32[128]{0:T(128)S(1)} all-reduce(f32[128]{0:T(128)S(1)} %reduce_sum.9), channel_id=1, replica_groups=mesh['row'=32,'col'=8] {'row','col'}, use_global_device_ids=true, to_apply=%region_4.0 | all-reduce | flops 128 | bytes 1024 | tf_op jit(solution)/shard_map/psum | solution.py:57
  173.2 0.5 broadcast_multiply_fusion.1
  173.7 207.5 %all-reduce.6.cloned.1.call-done = f32[128,2048]{0,1:T(8,128)} async-done(((f32[128,2048]{0,1:T(8,128)}), f32[128,2048]{0,1:T(8,128)}) %all-reduce.6.cloned.1.call-update) | async-done | bytes 1048592
  381.3 1.6 constant_dynamic-slice_fusion
  382.8 0.9 copy.25
  383.8 0.4 reshape.27
  384.1 5.0 convolution_multiply_fusion
  389.2 11.4 %reshape.28 = f32[16,32,64,32]{3,2,1,0:T(8,128)} reshape(f32[512,2048]{1,0:T(8,128)} %convolution_multiply_fusion) | data formatting | bytes 8388608 | tf_op jit(solution)/shard_map/reshape | solution.py:33
  400.6 12.7 %copy.33 = f32[32,32,16,64]{3,1,0,2:T(8,128)} copy(f32[32,32,16,64]{1,3,0,2:T(8,128)} %bitcast.43) | data formatting | bytes 8388608 | tf_op jit(solution)/shard_map/icje,ijz->cez/dot_general | solution.py:53
  413.3 9.9 %convolution_bitcast_fusion.2 = f32[1024,128]{1,0:T(8,128)} fusion(f32[1024,16,64]{2,0,1:T(8,128)} %bitcast.44, f32[16,64,128]{2,1,0:T(8,128)S(1)} %copy-done.1), kind=kOutput, calls=%fused_computation.5 | convolution fusion | flops 1610612736 | bytes 5242880 | tf_op jit(solution)/shard_map/icje,ijz->cez/dot_general | solution.py:53
  423.5 5.2 fusion.2
  428.7 0.8 copy.29
  429.6 17.6 %fusion.1 = f32[16,64,128]{2,1,0:T(8,128)} fusion(f32[16,32,64,32]{3,2,1,0:T(8,128)} %reshape.28, f32[32,32,128,1]{2,1,0,3:T(8,128)S(1)} %bitcast.41, f32[128]{0:T(128)S(1)} %copy-done.3), kind=kOutput, calls=%fused_computation.6 | convolution fusion | flops 1610743808 | bytes 5243392 | tf_op jit(solution)/shard_map/icje,cez->ijz/dot_general | solution.py:34
  447.2 235.7 %all-reduce.4.cloned.1.call-done = f32[1024,128]{1,0:T(8,128)} async-done(((f32[1024,128]{1,0:T(8,128)}), f32[1024,128]{1,0:T(8,128)}) %all-reduce.4.cloned.1.call-update) | async-done | bytes 524304 | tf_op jit(solution)/shard_map/psum | solution.py:57
  682.9 1.9 broadcast_multiply_fusion
  684.7 40.3 %reduce-scatter.5.cloned.1.call-done = f32[16,512]{1,0:T(8,128)} async-done(((f32[128,512]{1,0:T(8,128)}), f32[16,512]{1,0:T(8,128)}) %reduce-scatter.5.cloned.1.call-update) | async-done | bytes 32784
  (18 shorter events, 0.6 us)
Async XLA Ops:
  8.0 13.9 %copy-start = (f32[1024,128]{1,0:T(8,128)S(1)}, f32[1024,128]{1,0:T(8,128)}, u32[]{:S(2)}) copy-start(f32[1024,128]{1,0:T(8,128)} %param.7) | copy-start | bytes 1572868
  10.1 373.7 %all-to-all-start = ((f32[32,4,2048]{2,1,0:T(4,128)}), f32[32,4,2048]{2,1,0:T(4,128)S(1)}, u32[]{:S(2)}, u32[]{:S(2)}) async-start(f32[32,4,2048]{2,1,0:T(4,128)} %stack.2), calls=%async_computation | async-start | bytes 2097152 | tf_op jit(solution)/shard_map/all_to_all | solution.py:21
  21.8 359.5 %all-reduce.6.cloned.1.call-start = ((), (), s32[]{:S(2)}) async-start(), calls=%async_computation.4 | async-start | bytes 2097152
  44.0 13.5 %copy-start.2 = (f32[16,512]{1,0:T(8,128)S(1)}, f32[16,512]{1,0:T(8,128)}, u32[]{:S(2)}) copy-start(f32[16,512]{1,0:T(8,128)} %param.5) | copy-start | bytes 98308
  44.0 52.0 %copy-start.1 = (f32[16,64,128]{2,1,0:T(8,128)S(1)}, f32[16,64,128]{2,1,0:T(8,128)}, u32[]{:S(2)}) copy-start(f32[16,64,128]{2,1,0:T(8,128)} %param.9) | copy-start | bytes 1572868
  44.0 52.2 %copy-start.4 = (u32[256]{0:T(256)S(1)}, u32[256]{0:T(256)}, u32[]{:S(2)}) copy-start(u32[256]{0:T(256)} %constant.18) | copy-start | bytes 3076
  96.0 586.9 %all-reduce.4.cloned.1.call-start = ((), (), s32[]{:S(2)}) async-start(), calls=%async_computation.2 | async-start | bytes 1048576 | tf_op jit(solution)/shard_map/psum | solution.py:57
  413.3 16.3 %copy-start.3 = (f32[128]{0:T(128)S(1)}, f32[128]{0:T(128)}, u32[]{:S(2)}) copy-start(f32[128]{0:T(128)} %param.8) | copy-start | bytes 1540
  423.2 301.8 %reduce-scatter.5.cloned.1.call-start = ((), (), s32[]{:S(2)}) async-start(), calls=%async_computation.3 | async-start | bytes 294912
Sparse Core Ops, SparseCore 0:
  96.1 285.1 all-reduce.5
Sparse Core Ops, SparseCore 1:
  423.3 259.5 all-reduce.3
  685.8 39.2 reduce-scatter.4
